TPU v7x, 512 devices: a whole 4x8x8 slice. The times are simulated.
512 devices in a mesh: ha: 8 (over y_lo, core), az: 64 (over x, z, y_hi).
Axes of the slice: x: 4, y: 8 (y_hi: 2, y_lo: 4; y = y_hi * 4 + y_lo), z: 8, core: 2. Of those that a mesh axis runs over, the one named last changes fastest.
Arguments:
- field: float32 [2, 4096, 8192], P(None, 'ha', 'az'), may hold values from -6 to 6
- terrain: int32 [8192], P('az'), may hold values from 0 to 63
- profile_pick: int32 [8192], P('az'), may hold values from 0 to 15
- profile_table: float32 [16, 4096], replicated, may hold values from -3.140625 to 3.140625
- clutter_mask: int32 [128, 8192], P(None, 'az'), may hold values 0 or 1
- pulse: float32 [63], replicated, may hold values from -0.6 to 0.6
- beam: float32 [31], replicated, may hold values from -0.9 to 0.9
- measured: float32 [2, 128, 8192], P(None, None, 'az'), may hold values from -6 to 6
Outputs:
- field_out: float32 [2, 4096, 8192], P(None, 'ha', 'az')
- sources: float32 [2, 2, 128, 8192], P(None, None, 'ha', 'az')
All inputs are finite; a program needn't handle non-finite values. No bound on the sum of `clutter_mask` on one device may be relied on, other than what follows from the above.
Results may differ from a plain program's by a relative error of at most 0.00022.
Values sent between devices are 32-bit elements; how exact they have to be, the bound alone decides.
No kernel may reach another device: no remote copies, remote signals or barrier semaphores. Data moves between devices by JAX's collectives and lax.ppermute only.
A program may use at most 64 MiB of HBM per device.

v0:
```python
import math
import jax
import jax.numpy as jnp
from jax import lax
from jax.sharding import PartitionSpec as P

height_chirp = 1
azimuth_chirp = 3


def broadcast(block, axis, owner):
    block = jnp.where(lax.axis_index(axis) == owner, block, jnp.zeros_like(block))
    return lax.psum(block, axis)


def with_halo(cells, sides, width):
    for axis, dim in sides:
        count = lax.axis_size(axis)
        head = lax.slice_in_dim(cells, 0, width, axis=dim)
        tail = lax.slice_in_dim(cells, cells.shape[dim] - width, cells.shape[dim], axis=dim)
        cells = jnp.concatenate(
            [
                lax.ppermute(tail, axis, [(i, (i + 1) % count) for i in range(count)]),
                cells,
                lax.ppermute(head, axis, [((i + 1) % count, i) for i in range(count)]),
            ],
            axis=dim,
        )
    return cells


def factors(count):
    first = 1
    probe = 1
    while probe * probe <= count:
        if count % probe == 0:
            first = probe
        probe += 1
    return (first, count // first)


def unit_roots(rows, cols, modulus):
    left = lax.broadcasted_iota(jnp.int32, (rows, cols), 0)
    right = lax.broadcasted_iota(jnp.int32, (rows, cols), 1)
    turn = (left * right % modulus).astype(jnp.float32) * (2.0 * math.pi / modulus)
    return (jnp.cos(turn), -jnp.sin(turn))


def chirp_table(first, second, spread, count):
    low = lax.broadcasted_iota(jnp.int32, (first, second), 0)
    high = lax.broadcasted_iota(jnp.int32, (first, second), 1)
    index = low + first * high
    angle = (spread * index * index % (2 * count)).astype(jnp.float32) * (-math.pi / count)
    return (jnp.cos(angle), jnp.sin(angle))


def complex_table(table_re, table_im):
    return jnp.stack([jnp.stack([table_re, -table_im]), jnp.stack([table_im, table_re])])


def cmul(left_re, left_im, right_re, right_im):
    return (left_re * right_re - left_im * right_im, left_re * right_im + left_im * right_re)


def stacked_mul(vals, table_re, table_im):
    new_re, new_im = cmul(vals[0], vals[1], table_re, table_im)
    return jnp.stack([new_re, new_im])


def propagate(part_re, part_im, spread):
    highest = lax.Precision.HIGHEST
    count = part_re.shape[1]
    first, second = factors(count)
    split = (part_re.shape[0], first, second)
    table_shape = (1, first, second)
    outer_re, outer_im = unit_roots(first, first, first)
    inner_re, inner_im = unit_roots(second, second, second)
    twist_re, twist_im = unit_roots(first, second, count)
    twist_re = twist_re.reshape(table_shape)
    twist_im = twist_im.reshape(table_shape)
    phase_re, phase_im = chirp_table(first, second, spread, count)
    phase_re = phase_re.reshape(table_shape)
    phase_im = phase_im.reshape(table_shape)
    outer_fwd = complex_table(outer_re, outer_im)
    inner_fwd = complex_table(inner_re, inner_im)
    inner_inv = complex_table(inner_re.T, -inner_im.T)
    outer_inv = complex_table(outer_re.T, -outer_im.T)
    vals = jnp.stack([part_re.reshape(split), part_im.reshape(split)])
    vals = jnp.einsum("ocka,clab->olkb", outer_fwd, vals, precision=highest)
    vals = stacked_mul(vals, twist_re, twist_im)
    vals = jnp.einsum("clkb,ocbq->olkq", vals, inner_fwd, precision=highest)
    vals = stacked_mul(vals, phase_re, phase_im)
    vals = jnp.einsum("clkq,ocqb->olkb", vals, inner_inv, precision=highest)
    vals = stacked_mul(vals, twist_re, -twist_im)
    vals = jnp.einsum("ocak,clkb->olab", outer_inv, vals, precision=highest)
    scale = 1.0 / count
    return ((vals[0] * scale).reshape(part_re.shape), (vals[1] * scale).reshape(part_im.shape))


def screen_coef(rows, terr, phase, total):
    height = rows.astype(jnp.float32)
    depth = jnp.maximum(height - 0.75 * total, 0.0) / (0.25 * total)
    amount = jnp.exp(-4.0 * depth * depth) * (rows >= terr).astype(jnp.float32)
    return (amount * jnp.cos(phase), amount * jnp.sin(phase))


def onehot_of(picks, count):
    return (picks[None, :] == lax.broadcasted_iota(jnp.int32, (count, picks.shape[0]), 0)).astype(
        jnp.float32
    )


def lookup(table, picks):
    return jnp.einsum(
        "pr,pc->rc", table, onehot_of(picks, table.shape[0]), precision=lax.Precision.HIGHEST
    )


def band(taps, offset):
    hit = offset[:, :, None] == lax.broadcasted_iota(jnp.int32, (1, 1, taps.shape[0]), 2)
    return jnp.sum(jnp.where(hit, taps[None, None, :], 0.0), axis=-1)


def apply_screen(wave, coef):
    new_re, new_im = cmul(wave[0], wave[1], coef[0], coef[1])
    return jnp.stack([new_re, new_im])


def turn_rows(rows):
    new_re, new_im = propagate(rows[0], rows[1], azimuth_chirp)
    return jnp.stack([new_re, new_im])


def turn_items(block):
    return turn_rows(block[:, 0])[:, None]


def to_rows(wave):
    n_az = lax.axis_size("az")
    h_dev = wave.shape[1]
    part_rows = h_dev // n_az
    shaped = wave.reshape(2, n_az, part_rows, wave.shape[2])
    moved = turn_items(lax.all_to_all(shaped, "az", split_axis=1, concat_axis=3, tiled=True))
    return moved.reshape(2, part_rows, moved.shape[3])


def rows_to_slab(rows):
    return lax.all_to_all(rows, "az", split_axis=2, concat_axis=1, tiled=True)


def across(wave):
    return rows_to_slab(to_rows(wave))


def to_tall(wave):
    flipped = jnp.swapaxes(wave, 1, 2)
    return lax.all_to_all(flipped, "ha", split_axis=1, concat_axis=2, tiled=True)


def to_slab(tall):
    flipped = lax.all_to_all(tall, "ha", split_axis=2, concat_axis=1, tiled=True)
    return jnp.swapaxes(flipped, 1, 2)


def down(tall):
    new_re, new_im = propagate(tall[0], tall[1], height_chirp)
    return jnp.stack([new_re, new_im])


def root_strip(wave, bottom):
    return broadcast(wave[:, :bottom, :], "ha", 0)


def beam_forward(values, half_beam, forward_band):
    wider = with_halo(values, (("az", 1),), half_beam)
    return jnp.dot(wider, forward_band, precision=lax.Precision.HIGHEST)


def beam_backward(values, half_beam, back_band):
    wider = with_halo(values, (("az", 1),), half_beam)
    return jnp.dot(wider, back_band, precision=lax.Precision.HIGHEST)


def local(field, terrain, profile_pick, profile_table, clutter_mask, pulse, beam, measured):
    highest = lax.Precision.HIGHEST
    n_slabs = lax.axis_size("ha")
    h_dev = field.shape[1]
    a_dev = field.shape[2]
    total_h = h_dev * n_slabs
    slab = lax.axis_index("ha")
    bottom = clutter_mask.shape[0]
    share_rows = bottom // n_slabs
    row_start = slab * share_rows
    mask = clutter_mask.astype(jnp.float32)
    taps_range = pulse.shape[0]
    half_range = (taps_range - 1) // 2
    row_grid = lax.broadcasted_iota(jnp.int32, (bottom, bottom), 0)
    col_grid = lax.broadcasted_iota(jnp.int32, (bottom, bottom), 1)
    rmat = band(pulse, col_grid - row_grid + half_range)
    half_beam = (beam.shape[0] - 1) // 2
    wide = a_dev + 2 * half_beam
    edge = lax.broadcasted_iota(jnp.int32, (wide, a_dev), 0)
    column = lax.broadcasted_iota(jnp.int32, (wide, a_dev), 1)
    forward_band = band(beam, edge - column)
    back_band = band(beam, column - edge + 2 * half_beam)
    slab_rows = slab * h_dev + lax.broadcasted_iota(jnp.int32, (h_dev, 1), 0)
    slab_phase = lookup(
        lax.dynamic_slice_in_dim(profile_table, slab * h_dev, h_dev, 1), profile_pick
    )
    slab_coef = screen_coef(slab_rows, terrain[None, :], slab_phase, total_h)
    steps_count = measured.shape[0]
    wave = field
    result = []
    for step in range(steps_count):
        wave = to_slab(down(to_tall(across(wave))))
        wave = apply_screen(wave, slab_coef)
        strip = root_strip(wave, bottom)
        low_re = strip[0]
        low_im = strip[1]
        power = mask * (low_re * low_re + low_im * low_im)
        target = measured[step]
        ranged = jnp.dot(rmat, power, precision=highest)
        model = beam_forward(ranged, half_beam, forward_band)
        misfit = model - target
        spread_back = beam_backward(misfit, half_beam, back_band)
        back = jnp.einsum("pr,pa->ra", rmat, spread_back, precision=highest)
        whole = jnp.stack([2.0 * mask * low_re * back, 2.0 * mask * low_im * back])
        result.append(lax.dynamic_slice_in_dim(whole, row_start, share_rows, 1))
    return (wave, jnp.stack(result))


def solution(mesh):
    return jax.shard_map(
        local,
        mesh=mesh,
        in_specs=(
            P(None, "ha", "az"),
            P("az"),
            P("az"),
            P(),
            P(None, "az"),
            P(),
            P(),
            P(None, None, "az"),
        ),
        out_specs=(P(None, "ha", "az"), P(None, None, "ha", "az")),
        check_vma=False,
    )
```

profile of v0, /device:TPU:8, one launch (start us, length us, event | category | flops | bytes accessed | tf_op | source)
XLA Modules:
  0.0 512.8 jit_solution(6664515977165057099)
XLA Ops:
  9.1 18.1 %all-to-all-start = ((f32[2,64,8,128]{3,2,0,1:T(8,128)}), f32[2,64,8,128]{3,2,0,1:T(8,128)S(1)}, u32[]{:S(2)}, u32[]{:S(2)}) async-start(f32[2,64,8,128]{3,2,0,1:T(8,128)} %copy.267), calls=%async_computation | async-start | bytes 1048576 | tf_op jit(solution)/shard_map/all_to_all | solution.py:143
  28.6 21.4 %all-to-all-done = f32[2,64,8,128]{3,2,0,1:T(8,128)S(1)} async-done(((f32[2,64,8,128]{3,2,0,1:T(8,128)}), f32[2,64,8,128]{3,2,0,1:T(8,128)S(1)}, u32[]{:S(2)}, u32[]{:S(2)}) %all-to-all-start) | async-done | bytes 524320 | tf_op jit(solution)/shard_map/all_to_all | solution.py:143
  53.2 7.7 %copy.272 = f32[2,8,8192]{1,0,2:T(2,128)} copy(f32[2,8,8192]{2,1,0:T(8,128)S(1)} %pad_maximum_fusion.1) | data formatting | bytes 1048576 | tf_op jit(solution)/shard_map/stack | solution.py:131
  60.9 13.0 %reshape.559 = f32[64,1,2048]{2,1,0:T(1,128)S(1)} reshape(f32[8192,2,8]{2,1,0:T(2,128)} %bitcast.382) | data formatting | bytes 1048576
  73.8 27.5 %all_to_all.132 = f32[64,1,2048]{2,1,0:T(1,128)S(1)} all-to-all(f32[64,1,2048]{2,1,0:T(1,128)S(1)} %reshape.559), channel_id=1, replica_groups=mesh['ha'=8,'az'=64] {'az'}, dimensions={0} | all-to-all | bytes 1048576 | tf_op jit(solution)/shard_map/all_to_all | solution.py:148
  103.8 14.1 %reshape.560 = f32[8192,2,8]{2,1,0:T(2,128)} reshape(f32[64,2048]{1,0:T(8,128)S(1)} %reduce) | data formatting | bytes 1048576
  117.9 9.2 %copy.365 = f32[2,8,64,128]{3,1,2,0:T(8,128)S(1)} copy(f32[2,8,64,128]{1,0,3,2:T(2,128)} %bitcast.383) | data formatting | bytes 1048576 | tf_op jit(solution)/shard_map/all_to_all | solution.py:148
  132.0 11.4 %all-to-all-done.2 = f32[2,128,512]{2,0,1:T(2,128)S(1)} async-done(((f32[2,128,512]{2,0,1:T(2,128)}), f32[2,128,512]{2,0,1:T(2,128)S(1)}, u32[]{:S(2)}, u32[]{:S(2)}) %all-to-all-start.2) | async-done | bytes 524320 | tf_op jit(solution)/shard_map/all_to_all | solution.py:157
  154.6 7.9 %reshape.561 = f32[8,1,16384]{2,1,0:T(1,128)} reshape(f32[4096,2,16]{2,1,0:T(2,128)} %bitcast.386) | data formatting | bytes 1048576
  169.5 12.1 %all-to-all-done.3 = f32[8,1,16384]{2,1,0:T(1,128)S(1)} async-done(((f32[8,1,16384]{2,1,0:T(1,128)}), f32[8,1,16384]{2,1,0:T(1,128)S(1)}, u32[]{:S(2)}, u32[]{:S(2)}) %all-to-all-start.3) | async-done | bytes 524320 | tf_op jit(solution)/shard_map/all_to_all | solution.py:161
  197.8 26.0 %all_to_all.133 = f32[2,64,8,128]{3,2,0,1:T(8,128)S(1)} all-to-all(f32[2,64,8,128]{3,2,0,1:T(8,128)S(1)} %pad_maximum_fusion.3), channel_id=1, replica_groups=mesh['ha'=8,'az'=64] {'az'}, dimensions={1} | all-to-all | bytes 1048576 | tf_op jit(solution)/shard_map/all_to_all | solution.py:143
  227.0 7.7 %copy.298 = f32[2,8,8192]{1,0,2:T(2,128)} copy(f32[2,8,8192]{2,1,0:T(8,128)S(1)} %pad_maximum_fusion.4) | data formatting | bytes 1048576 | tf_op jit(solution)/shard_map/stack | solution.py:131
  234.7 13.0 %reshape.563 = f32[64,1,2048]{2,1,0:T(1,128)S(1)} reshape(f32[8192,2,8]{2,1,0:T(2,128)} %bitcast.384) | data formatting | bytes 1048576
  247.7 30.4 %all_to_all.134 = f32[64,1,2048]{2,1,0:T(1,128)S(1)} all-to-all(f32[64,1,2048]{2,1,0:T(1,128)S(1)} %reshape.563), channel_id=1, replica_groups=mesh['ha'=8,'az'=64] {'az'}, dimensions={0} | all-to-all | bytes 1048576 | tf_op jit(solution)/shard_map/all_to_all | solution.py:148
  280.0 14.1 %reshape.564 = f32[8192,2,8]{2,1,0:T(2,128)} reshape(f32[64,2048]{1,0:T(8,128)S(1)} %reduce.2) | data formatting | bytes 1048576
  294.1 9.2 %copy.376 = f32[2,8,64,128]{3,1,2,0:T(8,128)S(1)} copy(f32[2,8,64,128]{1,0,3,2:T(2,128)} %bitcast.385) | data formatting | bytes 1048576 | tf_op jit(solution)/shard_map/all_to_all | solution.py:148
  303.5 17.0 %all_to_all.135 = f32[2,128,512]{2,0,1:T(2,128)S(1)} all-to-all(f32[2,128,512]{2,0,1:T(2,128)S(1)} %copy.301), channel_id=1, replica_groups=mesh['ha'=8,'az'=64] {'ha'}, dimensions={1} | all-to-all | bytes 1048576 | tf_op jit(solution)/shard_map/all_to_all | solution.py:157
  331.6 7.9 %reshape.565 = f32[8,1,16384]{2,1,0:T(1,128)} reshape(f32[4096,2,16]{2,1,0:T(2,128)} %bitcast.388) | data formatting | bytes 1048576
  347.0 10.4 %all-to-all-done.7 = f32[8,1,16384]{2,1,0:T(1,128)S(1)} async-done(((f32[8,1,16384]{2,1,0:T(1,128)}), f32[8,1,16384]{2,1,0:T(1,128)S(1)}, u32[]{:S(2)}, u32[]{:S(2)}) %all-to-all-start.7) | async-done | bytes 524320 | tf_op jit(solution)/shard_map/all_to_all | solution.py:161
  375.6 67.0 %all-reduce.3.cloned.1.call-done = (f32[2,128,128]{2,1,0:T(8,128)}, f32[2,128,128]{2,1,0:T(8,128)}) async-done(((f32[2,128,128]{2,1,0:T(8,128)}, f32[2,128,128]{2,1,0:T(8,128)}), (f32[2,128,128]{2,1,0:T(8,128)}, f32[2,128,128]{2,1,0:T(8,128)})) %all-reduce.3.cloned.1.call-update) | async-done | bytes 262160 | tf_op jit(solution)/shard_map/psum | solution.py:13
  449.6 9.3 %collective-permute-start.1 = (f32[128,15]{0,1:T(8,128)S(1)}, f32[128,15]{0,1:T(8,128)S(1)}, u32[]{:S(2)}, u32[]{:S(2)}) collective-permute-start(f32[128,15]{0,1:T(8,128)S(1)} %get-tuple-element.65), channel_id=1, source_target_pairs={{1,0},{2,1},{3,2},{4,3},{5,4},{6,5},{7,6},{8,7},{9,8},{10,9},{11,1... | collective-permute-start | bytes 23048 | tf_op jit(solution)/shard_map/ppermute | solution.py:25
  460.9 12.0 %collective-permute-start.5 = (f32[128,15]{0,1:T(8,128)S(1)}, f32[128,15]{0,1:T(8,128)S(1)}, u32[]{:S(2)}, u32[]{:S(2)}) collective-permute-start(f32[128,15]{0,1:T(8,128)S(1)} %get-tuple-element.69), channel_id=1, source_target_pairs={{1,0},{2,1},{3,2},{4,3},{5,4},{6,5},{7,6},{8,7},{9,8},{10,9},{11,1... | collective-permute-start | bytes 23048 | tf_op jit(solution)/shard_map/ppermute | solution.py:25
  475.3 12.0 %collective-permute-start.3 = (f32[128,15]{0,1:T(8,128)S(1)}, f32[128,15]{0,1:T(8,128)S(1)}, u32[]{:S(2)}, u32[]{:S(2)}) collective-permute-start(f32[128,15]{0,1:T(8,128)S(1)} %get-tuple-element.63), channel_id=1, source_target_pairs={{1,0},{2,1},{3,2},{4,3},{5,4},{6,5},{7,6},{8,7},{9,8},{10,9},{11,1... | collective-permute-start | bytes 23048 | tf_op jit(solution)/shard_map/ppermute | solution.py:25
  489.8 12.0 %collective-permute-start.7 = (f32[128,15]{0,1:T(8,128)S(1)}, f32[128,15]{0,1:T(8,128)S(1)}, u32[]{:S(2)}, u32[]{:S(2)}) collective-permute-start(f32[128,15]{0,1:T(8,128)S(1)} %get-tuple-element.67), channel_id=1, source_target_pairs={{1,0},{2,1},{3,2},{4,3},{5,4},{6,5},{7,6},{8,7},{9,8},{10,9},{11,1... | collective-permute-start | bytes 23048 | tf_op jit(solution)/shard_map/ppermute | solution.py:25
  (161 shorter events, 106.9 us)
Async XLA Ops:
  7.2 189.3 %copy-start = (f32[16,4096]{1,0:T(8,128)S(1)}, f32[16,4096]{1,0:T(8,128)}, u32[]{:S(2)}) copy-start(f32[16,4096]{1,0:T(8,128)} %param.11) | copy-start | bytes 786436
  9.1 40.9 %all-to-all-start = ((f32[2,64,8,128]{3,2,0,1:T(8,128)}), f32[2,64,8,128]{3,2,0,1:T(8,128)S(1)}, u32[]{:S(2)}, u32[]{:S(2)}) async-start(f32[2,64,8,128]{3,2,0,1:T(8,128)} %copy.267), calls=%async_computation | async-start | bytes 1048576 | tf_op jit(solution)/shard_map/all_to_all | solution.py:143
  128.0 15.4 %all-to-all-start.2 = ((f32[2,128,512]{2,0,1:T(2,128)}), f32[2,128,512]{2,0,1:T(2,128)S(1)}, u32[]{:S(2)}, u32[]{:S(2)}) async-start(f32[2,128,512]{2,0,1:T(2,128)} %copy.275), calls=%async_computation.2 | async-start | bytes 1048576 | tf_op jit(solution)/shard_map/all_to_all | solution.py:157
  162.4 19.2 %all-to-all-start.3 = ((f32[8,1,16384]{2,1,0:T(1,128)}), f32[8,1,16384]{2,1,0:T(1,128)S(1)}, u32[]{:S(2)}, u32[]{:S(2)}) async-start(f32[8,1,16384]{2,1,0:T(1,128)} %reshape.561), calls=%async_computation.3 | async-start | bytes 1048576 | tf_op jit(solution)/shard_map/all_to_all | solution.py:161
  183.5 12.9 %copy-start.4 = (s32[128]{0:T(128)S(1)}, s32[128]{0:T(128)}, u32[]{:S(2)}) copy-start(s32[128]{0:T(128)} %param.9) | copy-start | bytes 1540
  183.5 12.9 %copy-start.5 = (s32[128]{0:T(128)S(1)}, s32[128]{0:T(128)}, u32[]{:S(2)}) copy-start(s32[128]{0:T(128)} %param.10) | copy-start | bytes 1540
  327.2 18.2 %copy-start.3 = (f32[2,128,128]{2,1,0:T(8,128)S(1)}, f32[2,128,128]{2,1,0:T(8,128)}, u32[]{:S(2)}) copy-start(f32[2,128,128]{2,1,0:T(8,128)} %param.15) | copy-start | bytes 393220
  331.6 14.1 %copy-start.6 = (f32[31]{0:T(128)S(1)}, f32[31]{0:T(128)}, u32[]{:S(2)}) copy-start(f32[31]{0:T(128)} %param.14) | copy-start | bytes 376
  339.5 17.8 %all-to-all-start.7 = ((f32[8,1,16384]{2,1,0:T(1,128)}), f32[8,1,16384]{2,1,0:T(1,128)S(1)}, u32[]{:S(2)}, u32[]{:S(2)}) async-start(f32[8,1,16384]{2,1,0:T(1,128)} %reshape.565), calls=%async_computation.7 | async-start | bytes 1048576 | tf_op jit(solution)/shard_map/all_to_all | solution.py:161
  345.2 97.4 %all-reduce.3.cloned.1.call-start = ((), (), s32[]{:S(2)}) async-start(), calls=%async_computation.8 | async-start | bytes 524288 | tf_op jit(solution)/shard_map/psum | solution.py:13
  366.8 7.5 %copy-start.7 = (f32[63]{0:T(128)S(1)}, f32[63]{0:T(128)}, u32[]{:S(2)}) copy-start(f32[63]{0:T(128)} %param.13) | copy-start | bytes 760
  366.8 75.8 %copy-start.2 = (s32[128,128]{1,0:T(8,128)S(1)}, s32[128,128]{1,0:T(8,128)}, u32[]{:S(2)}) copy-start(s32[128,128]{1,0:T(8,128)} %param.12) | copy-start | bytes 196612
  366.8 138.7 %copy-start.1 = (f32[16,4096]{1,0:T(8,128)S(1)}, f32[16,4096]{1,0:T(8,128)}, u32[]{:S(2)}) copy-start(f32[16,4096]{1,0:T(8,128)} %param.11) | copy-start | bytes 786436
  444.9 28.0 %collective-permute-start = (f32[128,15]{0,1:T(8,128)S(1)}, f32[128,15]{0,1:T(8,128)S(1)}, u32[]{:S(2)}, u32[]{:S(2)}) collective-permute-start(f32[128,15]{0,1:T(8,128)S(1)} %get-tuple-element.64), channel_id=1, source_target_pairs={{0,1},{1,2},{2,3},{3,4},{4,5},{5,6},{6,7},{7,8},{8,9},{9,10},{10,1... | collective-permute-start | bytes 23048 | tf_op jit(solution)/shard_map/ppermute | solution.py:23
  449.6 23.4 %collective-permute-start.1 = (f32[128,15]{0,1:T(8,128)S(1)}, f32[128,15]{0,1:T(8,128)S(1)}, u32[]{:S(2)}, u32[]{:S(2)}) collective-permute-start(f32[128,15]{0,1:T(8,128)S(1)} %get-tuple-element.65), channel_id=1, source_target_pairs={{1,0},{2,1},{3,2},{4,3},{5,4},{6,5},{7,6},{8,7},{9,8},{10,9},{11,1... | collective-permute-start | bytes 23048 | tf_op jit(solution)/shard_map/ppermute | solution.py:25
  458.9 28.5 %collective-permute-start.4 = (f32[128,15]{0,1:T(8,128)S(1)}, f32[128,15]{0,1:T(8,128)S(1)}, u32[]{:S(2)}, u32[]{:S(2)}) collective-permute-start(f32[128,15]{0,1:T(8,128)S(1)} %get-tuple-element.68), channel_id=1, source_target_pairs={{0,1},{1,2},{2,3},{3,4},{4,5},{5,6},{6,7},{7,8},{8,9},{9,10},{10,1... | collective-permute-start | bytes 23048 | tf_op jit(solution)/shard_map/ppermute | solution.py:23
  460.9 26.5 %collective-permute-start.5 = (f32[128,15]{0,1:T(8,128)S(1)}, f32[128,15]{0,1:T(8,128)S(1)}, u32[]{:S(2)}, u32[]{:S(2)}) collective-permute-start(f32[128,15]{0,1:T(8,128)S(1)} %get-tuple-element.69), channel_id=1, source_target_pairs={{1,0},{2,1},{3,2},{4,3},{5,4},{6,5},{7,6},{8,7},{9,8},{10,9},{11,1... | collective-permute-start | bytes 23048 | tf_op jit(solution)/shard_map/ppermute | solution.py:25
  473.4 28.4 %collective-permute-start.2 = (f32[128,15]{0,1:T(8,128)S(1)}, f32[128,15]{0,1:T(8,128)S(1)}, u32[]{:S(2)}, u32[]{:S(2)}) collective-permute-start(f32[128,15]{0,1:T(8,128)S(1)} %get-tuple-element.62), channel_id=1, source_target_pairs={{0,1},{1,2},{2,3},{3,4},{4,5},{5,6},{6,7},{7,8},{8,9},{9,10},{10,1... | collective-permute-start | bytes 23048 | tf_op jit(solution)/shard_map/ppermute | solution.py:23
  475.3 26.5 %collective-permute-start.3 = (f32[128,15]{0,1:T(8,128)S(1)}, f32[128,15]{0,1:T(8,128)S(1)}, u32[]{:S(2)}, u32[]{:S(2)}) collective-permute-start(f32[128,15]{0,1:T(8,128)S(1)} %get-tuple-element.63), channel_id=1, source_target_pairs={{1,0},{2,1},{3,2},{4,3},{5,4},{6,5},{7,6},{8,7},{9,8},{10,9},{11,1... | collective-permute-start | bytes 23048 | tf_op jit(solution)/shard_map/ppermute | solution.py:25
  487.9 14.7 %collective-permute-start.6 = (f32[128,15]{0,1:T(8,128)S(1)}, f32[128,15]{0,1:T(8,128)S(1)}, u32[]{:S(2)}, u32[]{:S(2)}) collective-permute-start(f32[128,15]{0,1:T(8,128)S(1)} %get-tuple-element.66), channel_id=1, source_target_pairs={{0,1},{1,2},{2,3},{3,4},{4,5},{5,6},{6,7},{7,8},{8,9},{9,10},{10,1... | collective-permute-start | bytes 23048 | tf_op jit(solution)/shard_map/ppermute | solution.py:23
  489.8 13.4 %collective-permute-start.7 = (f32[128,15]{0,1:T(8,128)S(1)}, f32[128,15]{0,1:T(8,128)S(1)}, u32[]{:S(2)}, u32[]{:S(2)}) collective-permute-start(f32[128,15]{0,1:T(8,128)S(1)} %get-tuple-element.67), channel_id=1, source_target_pairs={{1,0},{2,1},{3,2},{4,3},{5,4},{6,5},{7,6},{8,7},{9,8},{10,9},{11,1... | collective-permute-start | bytes 23048 | tf_op jit(solution)/shard_map/ppermute | solution.py:25
Sparse Core Ops, SparseCore 0:
  374.4 68.1 all-reduce.2
where the time goes:
time: 522 us; the launch traced here: 513 us
  local copies, waits for them, and re-layouts  146 us (28%)
  waiting for transfers between devices  123 us (24%)
  blocking collectives  101 us (19%)
  starting transfers between devices  90.5 us (17%)
  matrix products  20.1 us (4%)
  other arithmetic  16.4 us (3%)
  between operations  15.5 us (3%)
    unnamed x26, local copies, waits for them, and re-layouts  85.3 us
    psum x1, waiting for transfers between devices, broadcast(): return lax.psum(block, axis)  67 us
    all_to_all x2, blocking collectives, rows_to_slab(): return lax.all_to_all(rows, 'az', split_axis=2, concat_axis=1, tiled=True)  57.9 us
    ppermute x4, starting transfers between devices, with_halo(): lax.ppermute(head, axis, [((i + 1) % count, i) for i in range(count)])  45.5 us
    all_to_all x1, blocking collectives, to_rows(): lax.all_to_all(shaped, 'az', split_axis=1, concat_axis=3, tiled=True)  26 us
    all_to_all x2, waiting for transfers between devices, to_slab(): lax.all_to_all(tall, 'ha', split_axis=2, concat_axis=1, tiled=True)  22.4 us
    all_to_all x1, waiting for transfers between devices, to_rows(): lax.all_to_all(shaped, 'az', split_axis=1, concat_axis=3, tiled=True)  21.4 us
    all_to_all x3, local copies, waits for them, and re-layouts, rows_to_slab(): return lax.all_to_all(rows, 'az', split_axis=2, concat_axis=1, tiled=True)  18.8 us
  transfers between devices with their start and end apart: 13, of which 6 were waited for; matrix products, arithmetic and copies ran while one was open for 1% of the time, Pallas kernels for 0%

commit v1 on v0

--- a/solution.py
+++ b/solution.py
@@ -158,7 +158,9 @@
 
 
 def to_slab(tall):
-    flipped = lax.all_to_all(tall, "ha", split_axis=2, concat_axis=1, tiled=True)
+    flipped = jnp.concatenate(
+        lax.all_to_all(jnp.stack(jnp.split(tall, lax.axis_size("ha"), axis=2)), "ha", 0, 0), axis=1
+    )
     return jnp.swapaxes(flipped, 1, 2)
 
 

time: 522 us -> 478 us (0.916)
  local copies, waits for them, and re-layouts: 146 us -> 107 us
    unnamed x26 -> x38, local copies, waits for them, and re-layouts: 85.3 us -> 63.3 us
    all_to_all x4 -> x0, local copies, waits for them, and re-layouts: 10.7 us -> none  [to_slab(): lax.all_to_all(tall, 'ha', split_axis=2, concat_axis=1, tiled=True)]
    another operation x2, local copies, waits for them, and re-layouts: 8.71 us -> 0.04 us  [down(): return jnp.stack([new_re, new_im])]
where the time goes in v1:
time: 478 us; the launch traced here: 469 us
  waiting for transfers between devices  123 us (26%)
  local copies, waits for them, and re-layouts  107 us (22%)
  blocking collectives  101 us (21%)
  starting transfers between devices  90.4 us (19%)
  matrix products  20.1 us (4%)
  between operations  15.4 us (3%)
  other arithmetic  12.6 us (3%)
    psum x1, waiting for transfers between devices, broadcast(): return lax.psum(block, axis)  66.8 us
    unnamed x38, local copies, waits for them, and re-layouts  63.3 us
    all_to_all x2, blocking collectives, rows_to_slab(): return lax.all_to_all(rows, 'az', split_axis=2, concat_axis=1, tiled=True)  58.6 us
    ppermute x4, starting transfers between devices, with_halo(): lax.ppermute(head, axis, [((i + 1) % count, i) for i in range(count)])  45.5 us
    all_to_all x1, blocking collectives, to_rows(): lax.all_to_all(shaped, 'az', split_axis=1, concat_axis=3, tiled=True)  25.8 us
    all_to_all x2, waiting for transfers between devices, to_slab(): lax.all_to_all(jnp.stack(jnp.split(tall, lax.axis_size('ha'), axis=2)), '...  22.4 us
    all_to_all x1, waiting for transfers between devices, to_rows(): lax.all_to_all(shaped, 'az', split_axis=1, concat_axis=3, tiled=True)  21.4 us
    all_to_all x3, local copies, waits for them, and re-layouts, rows_to_slab(): return lax.all_to_all(rows, 'az', split_axis=2, concat_axis=1, tiled=True)  18.8 us
  transfers between devices with their start and end apart: 13, of which 6 were waited for; matrix products, arithmetic and copies ran while one was open for 1% of the time, Pallas kernels for 0%

profile of v1, /device:TPU:8, one launch (start us, length us, event | category | flops | bytes accessed | tf_op | source)
XLA Modules:
  0.0 469.1 jit_solution(7722174558447490968)
XLA Ops:
  9.1 18.1 %all-to-all-start = ((f32[2,64,8,128]{3,2,0,1:T(8,128)}), f32[2,64,8,128]{3,2,0,1:T(8,128)S(1)}, u32[]{:S(2)}, u32[]{:S(2)}) async-start(f32[2,64,8,128]{3,2,0,1:T(8,128)} %copy.269), calls=%async_computation | async-start | bytes 1048576 | tf_op jit(solution)/shard_map/all_to_all | solution.py:143
  28.6 21.4 %all-to-all-done = f32[2,64,8,128]{3,2,0,1:T(8,128)S(1)} async-done(((f32[2,64,8,128]{3,2,0,1:T(8,128)}), f32[2,64,8,128]{3,2,0,1:T(8,128)S(1)}, u32[]{:S(2)}, u32[]{:S(2)}) %all-to-all-start) | async-done | bytes 524320 | tf_op jit(solution)/shard_map/all_to_all | solution.py:143
  53.2 7.7 %copy.274 = f32[2,8,8192]{1,0,2:T(2,128)} copy(f32[2,8,8192]{2,1,0:T(8,128)S(1)} %pad_maximum_fusion.1) | data formatting | bytes 1048576 | tf_op jit(solution)/shard_map/stack | solution.py:131
  60.9 13.0 %reshape.575 = f32[64,1,2048]{2,1,0:T(1,128)S(1)} reshape(f32[8192,2,8]{2,1,0:T(2,128)} %bitcast.436) | data formatting | bytes 1048576
  73.9 27.8 %all_to_all.106 = f32[64,1,2048]{2,1,0:T(1,128)S(1)} all-to-all(f32[64,1,2048]{2,1,0:T(1,128)S(1)} %reshape.575), channel_id=1, replica_groups=mesh['ha'=8,'az'=64] {'az'}, dimensions={0} | all-to-all | bytes 1048576 | tf_op jit(solution)/shard_map/all_to_all | solution.py:148
  104.1 14.1 %reshape.576 = f32[8192,2,8]{2,1,0:T(2,128)} reshape(f32[64,2048]{1,0:T(8,128)S(1)} %reduce) | data formatting | bytes 1048576
  118.2 9.2 %copy.363 = f32[2,8,64,128]{3,1,2,0:T(8,128)S(1)} copy(f32[2,8,64,128]{1,0,3,2:T(2,128)} %bitcast.437) | data formatting | bytes 1048576 | tf_op jit(solution)/shard_map/all_to_all | solution.py:148
  132.4 11.4 %all-to-all-done.2 = f32[2,128,512]{2,0,1:T(2,128)S(1)} async-done(((f32[2,128,512]{2,0,1:T(2,128)}), f32[2,128,512]{2,0,1:T(2,128)S(1)}, u32[]{:S(2)}, u32[]{:S(2)}) %all-to-all-start.2) | async-done | bytes 524320 | tf_op jit(solution)/shard_map/all_to_all | solution.py:157
  155.7 6.8 %all-to-all-start.3 = ((f32[8,2,16,512]{3,2,1,0:T(8,128)}), f32[8,2,16,512]{3,2,1,0:T(8,128)S(1)}, u32[]{:S(2)}, u32[]{:S(2)}) async-start(f32[8,2,16,512]{3,2,1,0:T(8,128)} %fusion.78), calls=%async_computation.3 | async-start | bytes 1048576 | tf_op jit(solution)/shard_map/all_to_all | solution.py:162
  162.5 12.1 %all-to-all-done.3 = f32[8,2,16,512]{3,2,1,0:T(8,128)S(1)} async-done(((f32[8,2,16,512]{3,2,1,0:T(8,128)}), f32[8,2,16,512]{3,2,1,0:T(8,128)S(1)}, u32[]{:S(2)}, u32[]{:S(2)}) %all-to-all-start.3) | async-done | bytes 524320 | tf_op jit(solution)/shard_map/all_to_all | solution.py:162
  176.2 25.8 %all_to_all.107 = f32[2,64,8,128]{3,2,0,1:T(8,128)S(1)} all-to-all(f32[2,64,8,128]{3,2,0,1:T(8,128)S(1)} %pad_maximum_fusion.2), channel_id=1, replica_groups=mesh['ha'=8,'az'=64] {'az'}, dimensions={1} | all-to-all | bytes 1048576 | tf_op jit(solution)/shard_map/all_to_all | solution.py:143
  205.2 7.7 %copy.298 = f32[2,8,8192]{1,0,2:T(2,128)} copy(f32[2,8,8192]{2,1,0:T(8,128)S(1)} %pad_maximum_fusion.3) | data formatting | bytes 1048576 | tf_op jit(solution)/shard_map/stack | solution.py:131
  212.9 13.0 %reshape.577 = f32[64,1,2048]{2,1,0:T(1,128)S(1)} reshape(f32[8192,2,8]{2,1,0:T(2,128)} %bitcast.438) | data formatting | bytes 1048576
  225.9 30.7 %all_to_all.108 = f32[64,1,2048]{2,1,0:T(1,128)S(1)} all-to-all(f32[64,1,2048]{2,1,0:T(1,128)S(1)} %reshape.577), channel_id=1, replica_groups=mesh['ha'=8,'az'=64] {'az'}, dimensions={0} | all-to-all | bytes 1048576 | tf_op jit(solution)/shard_map/all_to_all | solution.py:148
  258.5 14.1 %reshape.578 = f32[8192,2,8]{2,1,0:T(2,128)} reshape(f32[64,2048]{1,0:T(8,128)S(1)} %reduce.1) | data formatting | bytes 1048576
  272.6 9.2 %copy.372 = f32[2,8,64,128]{3,1,2,0:T(8,128)S(1)} copy(f32[2,8,64,128]{1,0,3,2:T(2,128)} %bitcast.439) | data formatting | bytes 1048576 | tf_op jit(solution)/shard_map/all_to_all | solution.py:148
  282.0 16.7 %all_to_all.109 = f32[2,128,512]{2,0,1:T(2,128)S(1)} all-to-all(f32[2,128,512]{2,0,1:T(2,128)S(1)} %copy.301), channel_id=1, replica_groups=mesh['ha'=8,'az'=64] {'ha'}, dimensions={1} | all-to-all | bytes 1048576 | tf_op jit(solution)/shard_map/all_to_all | solution.py:157
  310.6 5.8 %all-to-all-start.7 = ((f32[8,2,16,512]{3,2,1,0:T(8,128)}), f32[8,2,16,512]{3,2,1,0:T(8,128)S(1)}, u32[]{:S(2)}, u32[]{:S(2)}) async-start(f32[8,2,16,512]{3,2,1,0:T(8,128)} %fusion.70), calls=%async_computation.7 | async-start | bytes 1048576 | tf_op jit(solution)/shard_map/all_to_all | solution.py:162
  318.2 10.4 %all-to-all-done.7 = f32[8,2,16,512]{3,2,1,0:T(8,128)S(1)} async-done(((f32[8,2,16,512]{3,2,1,0:T(8,128)}), f32[8,2,16,512]{3,2,1,0:T(8,128)S(1)}, u32[]{:S(2)}, u32[]{:S(2)}) %all-to-all-start.7) | async-done | bytes 524320 | tf_op jit(solution)/shard_map/all_to_all | solution.py:162
  332.2 66.8 %all-reduce.3.cloned.1.call-done = (f32[2,128,128]{2,1,0:T(8,128)}, f32[2,128,128]{2,1,0:T(8,128)}) async-done(((f32[2,128,128]{2,1,0:T(8,128)}, f32[2,128,128]{2,1,0:T(8,128)}), (f32[2,128,128]{2,1,0:T(8,128)}, f32[2,128,128]{2,1,0:T(8,128)})) %all-reduce.3.cloned.1.call-update) | async-done | bytes 262160 | tf_op jit(solution)/shard_map/psum | solution.py:13
  406.0 9.3 %collective-permute-start.1 = (f32[128,15]{0,1:T(8,128)S(1)}, f32[128,15]{0,1:T(8,128)S(1)}, u32[]{:S(2)}, u32[]{:S(2)}) collective-permute-start(f32[128,15]{0,1:T(8,128)S(1)} %get-tuple-element.65), channel_id=1, source_target_pairs={{1,0},{2,1},{3,2},{4,3},{5,4},{6,5},{7,6},{8,7},{9,8},{10,9},{11,1... | collective-permute-start | bytes 23048 | tf_op jit(solution)/shard_map/ppermute | solution.py:25
  417.3 12.0 %collective-permute-start.5 = (f32[128,15]{0,1:T(8,128)S(1)}, f32[128,15]{0,1:T(8,128)S(1)}, u32[]{:S(2)}, u32[]{:S(2)}) collective-permute-start(f32[128,15]{0,1:T(8,128)S(1)} %get-tuple-element.69), channel_id=1, source_target_pairs={{1,0},{2,1},{3,2},{4,3},{5,4},{6,5},{7,6},{8,7},{9,8},{10,9},{11,1... | collective-permute-start | bytes 23048 | tf_op jit(solution)/shard_map/ppermute | solution.py:25
  431.7 12.0 %collective-permute-start.3 = (f32[128,15]{0,1:T(8,128)S(1)}, f32[128,15]{0,1:T(8,128)S(1)}, u32[]{:S(2)}, u32[]{:S(2)}) collective-permute-start(f32[128,15]{0,1:T(8,128)S(1)} %get-tuple-element.63), channel_id=1, source_target_pairs={{1,0},{2,1},{3,2},{4,3},{5,4},{6,5},{7,6},{8,7},{9,8},{10,9},{11,1... | collective-permute-start | bytes 23048 | tf_op jit(solution)/shard_map/ppermute | solution.py:25
  446.2 12.0 %collective-permute-start.7 = (f32[128,15]{0,1:T(8,128)S(1)}, f32[128,15]{0,1:T(8,128)S(1)}, u32[]{:S(2)}, u32[]{:S(2)}) collective-permute-start(f32[128,15]{0,1:T(8,128)S(1)} %get-tuple-element.67), channel_id=1, source_target_pairs={{1,0},{2,1},{3,2},{4,3},{5,4},{6,5},{7,6},{8,7},{9,8},{10,9},{11,1... | collective-permute-start | bytes 23048 | tf_op jit(solution)/shard_map/ppermute | solution.py:25
  (171 shorter events, 66.4 us)
Async XLA Ops:
  7.2 167.7 %copy-start = (f32[16,4096]{1,0:T(8,128)S(1)}, f32[16,4096]{1,0:T(8,128)}, u32[]{:S(2)}) copy-start(f32[16,4096]{1,0:T(8,128)} %param.11) | copy-start | bytes 786436
  9.1 40.9 %all-to-all-start = ((f32[2,64,8,128]{3,2,0,1:T(8,128)}), f32[2,64,8,128]{3,2,0,1:T(8,128)S(1)}, u32[]{:S(2)}, u32[]{:S(2)}) async-start(f32[2,64,8,128]{3,2,0,1:T(8,128)} %copy.269), calls=%async_computation | async-start | bytes 1048576 | tf_op jit(solution)/shard_map/all_to_all | solution.py:143
  128.4 15.4 %all-to-all-start.2 = ((f32[2,128,512]{2,0,1:T(2,128)}), f32[2,128,512]{2,0,1:T(2,128)S(1)}, u32[]{:S(2)}, u32[]{:S(2)}) async-start(f32[2,128,512]{2,0,1:T(2,128)} %copy.277), calls=%async_computation.2 | async-start | bytes 1048576 | tf_op jit(solution)/shard_map/all_to_all | solution.py:157
  149.9 24.9 %copy-start.4 = (s32[128]{0:T(128)S(1)}, s32[128]{0:T(128)}, u32[]{:S(2)}) copy-start(s32[128]{0:T(128)} %param.9) | copy-start | bytes 1540
  149.9 24.9 %copy-start.5 = (s32[128]{0:T(128)S(1)}, s32[128]{0:T(128)}, u32[]{:S(2)}) copy-start(s32[128]{0:T(128)} %param.10) | copy-start | bytes 1540
  155.7 18.9 %all-to-all-start.3 = ((f32[8,2,16,512]{3,2,1,0:T(8,128)}), f32[8,2,16,512]{3,2,1,0:T(8,128)S(1)}, u32[]{:S(2)}, u32[]{:S(2)}) async-start(f32[8,2,16,512]{3,2,1,0:T(8,128)} %fusion.78), calls=%async_computation.3 | async-start | bytes 1048576 | tf_op jit(solution)/shard_map/all_to_all | solution.py:162
  304.6 12.1 %copy-start.3 = (f32[2,128,128]{2,1,0:T(8,128)S(1)}, f32[2,128,128]{2,1,0:T(8,128)}, u32[]{:S(2)}) copy-start(f32[2,128,128]{2,1,0:T(8,128)} %param.15) | copy-start | bytes 393220
  304.7 12.3 %copy-start.6 = (f32[31]{0:T(128)S(1)}, f32[31]{0:T(128)}, u32[]{:S(2)}) copy-start(f32[31]{0:T(128)} %param.14) | copy-start | bytes 376
  305.5 25.4 %copy-start.7 = (f32[63]{0:T(128)S(1)}, f32[63]{0:T(128)}, u32[]{:S(2)}) copy-start(f32[63]{0:T(128)} %param.13) | copy-start | bytes 760
  310.6 88.4 %copy-start.2 = (s32[128,128]{1,0:T(8,128)S(1)}, s32[128,128]{1,0:T(8,128)}, u32[]{:S(2)}) copy-start(s32[128,128]{1,0:T(8,128)} %param.12) | copy-start | bytes 196612
  310.6 18.0 %all-to-all-start.7 = ((f32[8,2,16,512]{3,2,1,0:T(8,128)}), f32[8,2,16,512]{3,2,1,0:T(8,128)S(1)}, u32[]{:S(2)}, u32[]{:S(2)}) async-start(f32[8,2,16,512]{3,2,1,0:T(8,128)} %fusion.70), calls=%async_computation.7 | async-start | bytes 1048576 | tf_op jit(solution)/shard_map/all_to_all | solution.py:162
  316.4 82.6 %all-reduce.3.cloned.1.call-start = ((), (), s32[]{:S(2)}) async-start(), calls=%async_computation.8 | async-start | bytes 524288 | tf_op jit(solution)/shard_map/psum | solution.py:13
  328.6 133.4 %copy-start.1 = (f32[16,4096]{1,0:T(8,128)S(1)}, f32[16,4096]{1,0:T(8,128)}, u32[]{:S(2)}) copy-start(f32[16,4096]{1,0:T(8,128)} %param.11) | copy-start | bytes 786436
  401.4 28.0 %collective-permute-start = (f32[128,15]{0,1:T(8,128)S(1)}, f32[128,15]{0,1:T(8,128)S(1)}, u32[]{:S(2)}, u32[]{:S(2)}) collective-permute-start(f32[128,15]{0,1:T(8,128)S(1)} %get-tuple-element.64), channel_id=1, source_target_pairs={{0,1},{1,2},{2,3},{3,4},{4,5},{5,6},{6,7},{7,8},{8,9},{9,10},{10,1... | collective-permute-start | bytes 23048 | tf_op jit(solution)/shard_map/ppermute | solution.py:23
  406.0 23.4 %collective-permute-start.1 = (f32[128,15]{0,1:T(8,128)S(1)}, f32[128,15]{0,1:T(8,128)S(1)}, u32[]{:S(2)}, u32[]{:S(2)}) collective-permute-start(f32[128,15]{0,1:T(8,128)S(1)} %get-tuple-element.65), channel_id=1, source_target_pairs={{1,0},{2,1},{3,2},{4,3},{5,4},{6,5},{7,6},{8,7},{9,8},{10,9},{11,1... | collective-permute-start | bytes 23048 | tf_op jit(solution)/shard_map/ppermute | solution.py:25
  415.4 28.5 %collective-permute-start.4 = (f32[128,15]{0,1:T(8,128)S(1)}, f32[128,15]{0,1:T(8,128)S(1)}, u32[]{:S(2)}, u32[]{:S(2)}) collective-permute-start(f32[128,15]{0,1:T(8,128)S(1)} %get-tuple-element.68), channel_id=1, source_target_pairs={{0,1},{1,2},{2,3},{3,4},{4,5},{5,6},{6,7},{7,8},{8,9},{9,10},{10,1... | collective-permute-start | bytes 23048 | tf_op jit(solution)/shard_map/ppermute | solution.py:23
  417.3 26.5 %collective-permute-start.5 = (f32[128,15]{0,1:T(8,128)S(1)}, f32[128,15]{0,1:T(8,128)S(1)}, u32[]{:S(2)}, u32[]{:S(2)}) collective-permute-start(f32[128,15]{0,1:T(8,128)S(1)} %get-tuple-element.69), channel_id=1, source_target_pairs={{1,0},{2,1},{3,2},{4,3},{5,4},{6,5},{7,6},{8,7},{9,8},{10,9},{11,1... | collective-permute-start | bytes 23048 | tf_op jit(solution)/shard_map/ppermute | solution.py:25
  429.8 28.4 %collective-permute-start.2 = (f32[128,15]{0,1:T(8,128)S(1)}, f32[128,15]{0,1:T(8,128)S(1)}, u32[]{:S(2)}, u32[]{:S(2)}) collective-permute-start(f32[128,15]{0,1:T(8,128)S(1)} %get-tuple-element.62), channel_id=1, source_target_pairs={{0,1},{1,2},{2,3},{3,4},{4,5},{5,6},{6,7},{7,8},{8,9},{9,10},{10,1... | collective-permute-start | bytes 23048 | tf_op jit(solution)/shard_map/ppermute | solution.py:23
  431.7 26.5 %collective-permute-start.3 = (f32[128,15]{0,1:T(8,128)S(1)}, f32[128,15]{0,1:T(8,128)S(1)}, u32[]{:S(2)}, u32[]{:S(2)}) collective-permute-start(f32[128,15]{0,1:T(8,128)S(1)} %get-tuple-element.63), channel_id=1, source_target_pairs={{1,0},{2,1},{3,2},{4,3},{5,4},{6,5},{7,6},{8,7},{9,8},{10,9},{11,1... | collective-permute-start | bytes 23048 | tf_op jit(solution)/shard_map/ppermute | solution.py:25
  444.3 14.7 %collective-permute-start.6 = (f32[128,15]{0,1:T(8,128)S(1)}, f32[128,15]{0,1:T(8,128)S(1)}, u32[]{:S(2)}, u32[]{:S(2)}) collective-permute-start(f32[128,15]{0,1:T(8,128)S(1)} %get-tuple-element.66), channel_id=1, source_target_pairs={{0,1},{1,2},{2,3},{3,4},{4,5},{5,6},{6,7},{7,8},{8,9},{9,10},{10,1... | collective-permute-start | bytes 23048 | tf_op jit(solution)/shard_map/ppermute | solution.py:23
  446.2 13.4 %collective-permute-start.7 = (f32[128,15]{0,1:T(8,128)S(1)}, f32[128,15]{0,1:T(8,128)S(1)}, u32[]{:S(2)}, u32[]{:S(2)}) collective-permute-start(f32[128,15]{0,1:T(8,128)S(1)} %get-tuple-element.67), channel_id=1, source_target_pairs={{1,0},{2,1},{3,2},{4,3},{5,4},{6,5},{7,6},{8,7},{9,8},{10,9},{11,1... | collective-permute-start | bytes 23048 | tf_op jit(solution)/shard_map/ppermute | solution.py:25
Sparse Core Ops, SparseCore 0:
  331.0 67.9 all-reduce.2
